TPU v7x, 32 devices: a whole 2x2x4 slice. The times are simulated.
32 devices in a mesh: facet: 4 (over z), col: 8 (over y, x, core).
Axes of the slice: x: 2, y: 2, z: 4, core: 2. Of those that a mesh axis runs over, the one named last changes fastest.
Arguments:
- sky_re: bfloat16 [4, 4096, 4096], P('facet', None, 'col'), may hold values from -6 to 6
- sky_im: bfloat16 [4, 4096, 4096], P('facet', None, 'col'), may hold values from -6 to 6
- col_offsets: int32 [2], replicated, may hold values from 0 to 65280
- sub_offsets: int32 [4], replicated, may hold values from 0 to 65280
- kernel: float32 [16, 8], replicated, may hold values from 0.05 to 1
- vis_count: int32 [4, 32], P('facet', 'col'), may hold values from 0 to 128, as said below
- cell_index: int32 [2, 4, 32, 128], P(None, 'facet', 'col'), may hold values from 0 to 248
- frac_index: int32 [2, 4, 32, 128], P(None, 'facet', 'col'), may hold values from 0 to 15
Outputs:
- vis_re: float32 [4, 32, 128], P('facet', 'col')
- vis_im: float32 [4, 32, 128], P('facet', 'col')
Inputs may be any that keep to these rules, and one draw needn't show every extreme that they name: Within each subgrid the blocks with visibilities come first and block 0 holds 128; in some subgrid all 32 blocks hold visibilities; a block's visibilities fill its first vis_count slots.
All inputs are finite; a program needn't handle non-finite values.
Results may differ from a plain program's by a relative error of at most 0.0037.
Values may be sent and summed in bfloat16 or wider, within the bound.
A program may use at most 64 MiB of HBM per device.

v0:
```python
import functools
import math

import jax
import jax.numpy as jnp
from jax import lax
from jax.experimental import pallas as pl
from jax.experimental.pallas import tpu as pltpu
from jax.sharding import PartitionSpec as P

N_IMG = 65536
MASK = N_IMG - 1
S = 256
SCOL = 2
LANES = 128
F32 = jnp.float32
BF16 = jnp.bfloat16


def unit(points):
    angles = points.astype(F32) * (2.0 * math.pi / N_IMG)
    return jnp.cos(angles), jnp.sin(angles)


def times(left, right):
    return (
        left[0] * right[0] - left[1] * right[1],
        left[0] * right[1] + left[1] * right[0],
    )


def iota(shape, dim):
    return lax.broadcasted_iota(jnp.int32, shape, dim)


def exclusive(left, right, count):
    total, bit = 0, 1
    while bit < count:
        total = total + ((left // bit) % 2 + (right // bit) % 2) % 2 * bit
        bit *= 2
    return total


def body(
    dims,
    coff_ref,
    soff_ref,
    kern_ref,
    count_ref,
    cell_ref,
    frac_ref,
    re_hbm,
    im_hbm,
    vis_ref,
    sky,
    table_a,
    table_b,
    prod,
    base,
    shift_tab,
    second,
    stacked,
    prod2,
    sendbuf,
    recv,
    zbuf,
    zrecv,
    grid,
    row_w,
    col_w,
    taps,
    sky_sem,
    send_sem,
    recv_sem,
    zsend_sem,
    zrecv_sem,
    gsend_sem,
    grecv_sem,
):
    n_f, n_c, pixels, cols, subs, owned, blocks, slots, groups, ksize, over = dims
    rows = S // groups
    rp = S // n_c
    dpg = n_c // groups
    per = subs // SCOL
    f = lax.axis_index("facet")
    c = lax.axis_index("col")

    loads = []
    for index, src in enumerate((re_hbm, im_hbm)):
        copy = pltpu.make_async_copy(
            src.at[0], sky.at[index], sky_sem.at[index]
        )
        copy.start()
        loads.append(copy)

    barrier = pltpu.get_barrier_semaphore()
    for step in range(1, n_c):
        pl.semaphore_signal(barrier, inc=1, device_id={"col": lax.rem(c + step, n_c)})
    for step in range(1, n_f):
        pl.semaphore_signal(barrier, inc=1, device_id={"facet": lax.rem(f + step, n_f)})

    jrow = iota((rows, LANES), 0)
    lane = iota((rows, LANES), 1)
    base[0], base[1] = unit(jrow * lane)
    base[2], base[3] = unit((jrow * LANES) & MASK)

    first_y = f * pixels + c * cols
    ycol = first_y + iota((subs, cols), 1)
    srow = iota((subs, cols), 0)
    soff = jnp.zeros((subs, cols), jnp.int32)
    for s in range(subs):
        soff = jnp.where(srow == s, soff_ref[s], soff)
    points = ((soff * (ycol // 256)) & MASK) * 256 + soff * (ycol % 256)
    shift_tab[0], shift_tab[1] = unit(points & MASK)

    strip = 32
    kline = iota((strip, S), 1)
    mline = first_y + iota((strip, S), 0)
    points = ((mline // 256 * kline) & MASK) * 256 + (mline % 256) * kline
    now = unit(points & MASK)
    scale2 = 1.0 / math.sqrt(pixels * n_f)
    now = (now[0] * scale2, now[1] * scale2)
    stride = unit((strip * iota((8, S), 1)) & MASK)
    stride = (stride[0][0:1], stride[1][0:1])
    for part in range(cols // strip):
        here = slice(part * strip, (part + 1) * strip)
        second[here, :S] = now[0].astype(BF16)
        second[here, S:] = now[1].astype(BF16)
        now = times(now, stride)

    own_group = c // dpg
    scale1 = 1.0 / math.sqrt(pixels)

    def send(dest):
        return pltpu.make_async_remote_copy(
            src_ref=sendbuf.at[dest],
            dst_ref=recv.at[c],
            send_sem=send_sem.at[dest],
            recv_sem=recv_sem.at[c],
            device_id={"col": dest},
        )

    def fill_table(table, g, columns):
        for q in columns:
            start = coff_ref[q] + g * rows
            ll = iota((8, LANES), 1)
            along = unit((start * ll) & MASK)
            along = (along[0][0:1] * scale1, along[1][0:1] * scale1)
            jump = unit((start * LANES + 0 * ll) & MASK)
            jump = (jump[0][0:1], jump[1][0:1])
            now = times((base[0], base[1]), along)
            jump = times((base[2], base[3]), jump)
            top = q * 2 * rows
            for part in range(pixels // LANES):
                lanes = slice(part * LANES, (part + 1) * LANES)
                table[top : top + rows, lanes] = now[0].astype(BF16)
                table[top + rows : top + 2 * rows, lanes] = now[1].astype(BF16)
                now = times(now, jump)

    def transform(table, g, prepare):
        for index in range(2):
            prepare(index)
            prod[:, index * cols : (index + 1) * cols] = jnp.dot(
                table[...], sky[index], preferred_element_type=F32
            )
        for q in range(SCOL):
            cos_rows = slice(q * 2 * rows, q * 2 * rows + rows)
            sin_rows = slice(q * 2 * rows + rows, (q + 1) * 2 * rows)
            band_re = prod[cos_rows, :cols] + prod[sin_rows, cols:]
            band_im = prod[cos_rows, cols:] - prod[sin_rows, :cols]
            band_re = band_re.astype(BF16).astype(F32)
            band_im = band_im.astype(BF16).astype(F32)
            for s in range(q * per, (q + 1) * per):
                sc = shift_tab[0, s : s + 1]
                sd = shift_tab[1, s : s + 1]
                at = s * 2 * rows
                stacked[at : at + rows] = (band_re * sc + band_im * sd).astype(BF16)
                stacked[at + rows : at + 2 * rows] = (band_im * sc - band_re * sd).astype(BF16)
        prod2[...] = jnp.dot(stacked[...], second[...], preferred_element_type=F32)
        for s in range(subs):
            for t in range(dpg):
                upper = slice(s * 2 * rows + t * rp, s * 2 * rows + (t + 1) * rp)
                lower = slice(upper.start + rows, upper.stop + rows)
                dest = g * dpg + t
                sendbuf[dest, s, :, :S] = (prod2[upper, :S] + prod2[lower, S:]).astype(BF16)
                sendbuf[dest, s, :, S:] = (prod2[lower, :S] - prod2[upper, S:]).astype(BF16)

    def group_at(step):
        return exclusive(own_group, groups - 1 - step, groups)

    tables = (table_a, table_b)
    fill_table(tables[0], group_at(0), range(SCOL))
    for step in range(groups):

        def prepare(index, step=step):
            if step == 0:
                loads[index].wait()
            if step + 1 < groups:
                fill_table(
                    tables[(step + 1) % 2], group_at(step + 1), range(index, SCOL, 2)
                )
            if index == 0 and step > 0:
                for t in range(dpg):
                    send(group_at(step - 1) * dpg + t).start()

        transform(tables[step % 2], group_at(step), prepare)
        if step == 0:
            pl.semaphore_wait(barrier, n_c - 1 + n_f - 1)

    total = owned * blocks
    frac = frac_ref[...]
    for tap in range(ksize):
        value = jnp.zeros(frac.shape, F32)
        for row in range(over):
            value = jnp.where(frac == row, kern_ref[tap, row], value)
        taps[tap] = value

    for t in range(dpg - 1):
        send(own_group * dpg + lax.rem(lax.rem(c, dpg) + 1 + t, dpg)).start()

    for b in range(total):
        lanes = slice(b * slots, (b + 1) * slots)
        away_row = iota((S, slots), 0) - cell_ref[b : b + 1]
        away_col = iota((S, slots), 0) - cell_ref[total + b : total + b + 1]
        row_val = jnp.zeros((S, slots), F32)
        col_val = jnp.zeros((S, slots), F32)
        for tap in range(ksize):
            row_val = jnp.where(away_row == tap, taps[tap, b : b + 1], row_val)
            col_val = jnp.where(away_col == tap, taps[tap, total + b : total + b + 1], col_val)
        row_w[:, lanes] = row_val.astype(BF16)
        col_w[:, lanes] = col_val

    for step in range(1, n_c):
        src = lax.rem(c + step, n_c)
        pltpu.make_async_remote_copy(
            src_ref=recv.at[src],
            dst_ref=recv.at[src],
            send_sem=send_sem.at[src],
            recv_sem=recv_sem.at[src],
            device_id={"col": src},
        ).wait_recv()
    for s in range(subs):
        acc = sendbuf[c, s].astype(F32)
        for step in range(1, n_c):
            acc = acc + recv[lax.rem(c + step, n_c), s].astype(F32)
        zbuf[s // owned, s % owned] = acc.astype(BF16)

    def zcopy(dest):
        return pltpu.make_async_remote_copy(
            src_ref=zbuf.at[dest],
            dst_ref=zrecv.at[f],
            send_sem=zsend_sem.at[dest],
            recv_sem=zrecv_sem.at[f],
            device_id={"facet": dest},
        )

    for step in range(1, n_f):
        zcopy(lax.rem(f + step, n_f)).start()
    for step in range(1, n_c):
        send(lax.rem(c + step, n_c)).wait_send()
    for step in range(1, n_f):
        src = lax.rem(f + step, n_f)
        pltpu.make_async_remote_copy(
            src_ref=zrecv.at[src],
            dst_ref=zrecv.at[src],
            send_sem=zsend_sem.at[src],
            recv_sem=zrecv_sem.at[src],
            device_id={"facet": src},
        ).wait_recv()
    acc = zbuf[f].astype(F32)
    for step in range(1, n_f):
        acc = acc + zrecv[lax.rem(f + step, n_f)].astype(F32)
    grid[c] = acc.astype(BF16)

    def gcopy(dest):
        return pltpu.make_async_remote_copy(
            src_ref=grid.at[c],
            dst_ref=grid.at[c],
            send_sem=gsend_sem.at[dest],
            recv_sem=grecv_sem.at[c],
            device_id={"col": dest},
        )

    for step in range(1, n_c):
        gcopy(lax.rem(c + step, n_c)).start()
    for step in range(1, n_f):
        zcopy(lax.rem(f + step, n_f)).wait_send()
    for step in range(1, n_c):
        src = lax.rem(c + step, n_c)
        pltpu.make_async_remote_copy(
            src_ref=grid.at[src],
            dst_ref=grid.at[src],
            send_sem=gsend_sem.at[src],
            recv_sem=grecv_sem.at[src],
            device_id={"col": src},
        ).wait_recv()
    for step in range(1, n_c):
        gcopy(lax.rem(c + step, n_c)).wait_send()

    for o in range(owned):
        cells = grid[:, o]
        if rp % 16 == 0:
            cells = cells.reshape(S, 2 * S)
        else:
            cells = cells.astype(F32).reshape(S, 2 * S).astype(BF16)
        for b in range(o * blocks, (o + 1) * blocks):
            lanes = slice(b * slots, (b + 1) * slots)
            summed = lax.dot_general(
                cells,
                row_w[:, lanes],
                (((0,), (0,)), ((), ())),
                preferred_element_type=F32,
            )
            weights = col_w[:, lanes]
            live = iota((1, slots), 1) < count_ref[b]
            vis_real = jnp.sum(summed[:S] * weights, axis=0, keepdims=True)
            vis_imag = jnp.sum(summed[S:] * weights, axis=0, keepdims=True)
            vis_ref[b : b + 1] = jnp.where(live, vis_real, 0.0)
            vis_ref[total + b : total + b + 1] = jnp.where(live, vis_imag, 0.0)


def local(sky_re, sky_im, col_offsets, sub_offsets, kernel, vis_count, cell_index, frac_index):
    n_f = lax.axis_size("facet")
    n_c = lax.axis_size("col")
    pixels, cols = sky_re.shape[1:]
    subs = sub_offsets.shape[0]
    owned, blocks = vis_count.shape
    slots = cell_index.shape[-1]
    over, ksize = kernel.shape
    groups = 4
    rows = S // groups
    rp = S // n_c
    total = owned * blocks
    dims = (n_f, n_c, pixels, cols, subs, owned, blocks, slots, groups, ksize, over)
    smem = pl.BlockSpec(memory_space=pltpu.SMEM)
    vmem = pl.BlockSpec(memory_space=pltpu.VMEM)
    anywhere = pl.BlockSpec(memory_space=pl.ANY)
    dma = pltpu.SemaphoreType.DMA
    out = jax.ShapeDtypeStruct((2 * total, slots), F32)
    vis = pl.pallas_call(
        functools.partial(body, dims),
        out_shape=out,
        in_specs=[smem, smem, smem, smem, vmem, vmem, anywhere, anywhere],
        out_specs=vmem,
        scratch_shapes=[
            pltpu.VMEM((2, pixels, cols), BF16),
            pltpu.VMEM((2 * SCOL * rows, pixels), BF16),
            pltpu.VMEM((2 * SCOL * rows, pixels), BF16),
            pltpu.VMEM((2 * SCOL * rows, 2 * cols), F32),
            pltpu.VMEM((4, rows, LANES), F32),
            pltpu.VMEM((2, subs, cols), F32),
            pltpu.VMEM((cols, 2 * S), BF16),
            pltpu.VMEM((2 * subs * rows, cols), BF16),
            pltpu.VMEM((2 * subs * rows, 2 * S), F32),
            pltpu.VMEM((n_c, subs, rp, 2 * S), BF16),
            pltpu.VMEM((n_c, subs, rp, 2 * S), BF16),
            pltpu.VMEM((n_f, owned, rp, 2 * S), BF16),
            pltpu.VMEM((n_f, owned, rp, 2 * S), BF16),
            pltpu.VMEM((n_c, owned, rp, 2 * S), BF16),
            pltpu.VMEM((S, total * slots), BF16),
            pltpu.VMEM((S, total * slots), F32),
            pltpu.VMEM((ksize, 2 * total, slots), F32),
            dma((2,)),
            dma((n_c,)),
            dma((n_c,)),
            dma((n_f,)),
            dma((n_f,)),
            dma((n_c,)),
            dma((n_c,)),
        ],
        compiler_params=pltpu.CompilerParams(
            collective_id=0, has_side_effects=True, vmem_limit_bytes=56 << 20
        ),
    )(
        col_offsets,
        sub_offsets,
        kernel.T,
        vis_count.reshape(total),
        cell_index.reshape(2 * total, slots),
        frac_index.reshape(2 * total, slots),
        sky_re,
        sky_im,
    )
    vis = vis.reshape(2, owned, blocks, slots)
    return (vis[0], vis[1])


def solution(mesh):
    placed = (
        P("facet", None, "col"),
        P("facet", None, "col"),
        P(),
        P(),
        P(),
        P("facet", "col"),
        P(None, "facet", "col", None),
        P(None, "facet", "col", None),
    )
    return jax.shard_map(
        local,
        mesh=mesh,
        in_specs=placed,
        out_specs=(P("facet", "col", None), P("facet", "col", None)),
        check_vma=False,
    )
```

profile of v0, /device:TPU:0, one launch (start us, length us, event | category | flops | bytes accessed | tf_op | source)
XLA Modules:
  0.0 35.5 jit_solution(2555268494972908926)
XLA Ops:
  0.6 33.5 %shard_map.95 = f32[8,128]{1,0:T(8,128)} custom-call(s32[2]{0:T(128)} %coff_ref.1, s32[4]{0:T(128)} %soff_ref.1, f32[8,16]{1,0:T(8,128)} %bitcast.8, s32[4]{0:T(128)} %bitcast.11, s32[8,128]{1,0:T(8,128)} %bitcast.9, s32[8,128]{1,0:T(8,128)} %bitcast.10, bf16[1,4096,512]{2,1,0:T(8,128)(2,1)} %re_hbm.1, bf16[1,4096,512]{2,1,0:T(8,128)(2,1)} %im_hbm.1), custom_call_target="tpu_custom_call" | custom-call | tf_op jit(solution)/shard_map/pallas_call | solution.py:340
  34.1 1.3 %slice_bitcast_fusion = (f32[1,4,128]{2,1,0:T(4,128)}, f32[1,4,128]{2,1,0:T(4,128)}) fusion(f32[8,128]{1,0:T(8,128)} %shard_map.95), kind=kLoop, calls=%fused_computation | loop fusion | bytes 8192 | tf_op jit(solution)/shard_map/squeeze | solution.py:385
where the time goes:
time: 35.7 us; the launch traced here: 35.5 us
  Pallas kernels  33.5 us (94%)
  local copies, waits for them, and re-layouts  1.33 us (4%)
  between operations  0.64 us (2%)
    pallas_call x1, Pallas kernels, local(): pl.pallas_call(functools.partial(body, dims), out_shape=out, in_specs=[sm...  33.5 us
    squeeze x1, local copies, waits for them, and re-layouts, local(): return (vis[0], vis[1])  1.33 us

commit v1 on v0

v1 whole, which is shorter than its diff:
```python
import functools
import math

import jax
import jax.numpy as jnp
from jax import lax
from jax.experimental import pallas as pl
from jax.experimental.pallas import tpu as pltpu
from jax.sharding import PartitionSpec as P

N_IMG = 65536
S = 256
SCOL = 2
LANES = 128
F32 = jnp.float32
BF16 = jnp.bfloat16


def iota(shape, dim):
    return lax.broadcasted_iota(jnp.int32, shape, dim)


def unit(points, period):
    quarter = period // 4
    quad = (points + quarter // 2) >> (quarter.bit_length() - 1)
    x = (points - quad * quarter).astype(F32) * (2.0 * math.pi / period)
    x2 = x * x
    s = x2 * (1.0 / 362880) - 1.0 / 5040
    s = x2 * s + 1.0 / 120
    s = x2 * s - 1.0 / 6
    s = x * (x2 * s + 1.0)
    c = x2 * (1.0 / 40320) - 1.0 / 720
    c = x2 * c + 1.0 / 24
    c = x2 * c - 0.5
    c = x2 * c + 1.0
    odd = (quad & 1) != 0
    cos = jnp.where(odd, s, c)
    sin = jnp.where(odd, c, s)
    cos = jnp.where(((quad + 1) & 2) != 0, -cos, cos)
    sin = jnp.where((quad & 2) != 0, -sin, sin)
    return cos, sin


def product(left, right, period):
    upper = (left * (right >> 8)) & (period - 1)
    return (upper * 256 + left * (right & 255)) & (period - 1)


def times(left, right):
    return (
        left[0] * right[0] - left[1] * right[1],
        left[0] * right[1] + left[1] * right[0],
    )


def exclusive(left, right, count):
    total, bit = 0, 1
    while bit < count:
        total = total + ((left // bit) % 2 + (right // bit) % 2) % 2 * bit
        bit *= 2
    return total


def each(count, step):
    if count <= 16:
        for index in range(count):
            step(index)
    else:

        def once(index, carry):
            step(index)
            return carry

        lax.fori_loop(0, count, once, 0)


def body(
    dims,
    coff_ref,
    soff_ref,
    kern_ref,
    count_ref,
    cell_ref,
    frac_ref,
    re_hbm,
    im_hbm,
    vis_ref,
    sky,
    table_a,
    table_b,
    state,
    prod,
    base,
    shift_tab,
    table2,
    stacked,
    bands,
    bsend,
    cells,
    idx,
    idx_all,
    row_r,
    row_t,
    col_r,
    col_t,
    weights,
    vsend,
    vrecv,
    sky_sem,
    band_sem,
    isend_sem,
    irecv_sem,
    vsend_sem,
    vrecv_sem,
):
    n_f, n_c, pixels, cols, subs, blocks, slots, chunks, ksize, over = dims
    per = subs // SCOL
    n_p = n_c // SCOL
    half = S // 2
    rows = 64
    f = lax.axis_index("facet")
    c = lax.axis_index("col")
    core = lax.rem(c, SCOL)
    chip = c // SCOL
    side = f // per
    depth = pixels // chunks

    loads = []
    for t in range(chunks):
        for index, src in enumerate((re_hbm, im_hbm)):
            copy = pltpu.make_async_copy(
                src.at[0, pl.ds(t * depth, depth)],
                sky.at[index, pl.ds(t * depth, depth)],
                sky_sem.at[t, index],
            )
            copy.start()
            loads.append(copy)

    barrier = pltpu.get_barrier_semaphore()
    everyone = n_f * n_c

    def greet(step):
        other = lax.rem(f * n_c + c + 1 + step, everyone)
        pl.semaphore_signal(
            barrier, inc=1, device_id={"facet": other // n_c, "col": lax.rem(other, n_c)}
        )

    each(everyone - 1, greet)

    jrow = iota((rows, LANES), 0)
    lane = iota((rows, LANES), 1)
    base[0], base[1] = unit(jrow * lane, N_IMG)
    base[2], base[3] = unit(jrow * LANES, N_IMG)
    scale1 = 1.0 / math.sqrt(pixels)

    def fill_table(table, q, t):
        parts = depth // LANES
        for g in range(S // rows):
            start = coff_ref[q] + g * rows
            ll = iota((8, LANES), 1)
            jump = unit((start * LANES + 0 * ll) & (N_IMG - 1), N_IMG)
            jump = times((base[2], base[3]), (jump[0][0:1], jump[1][0:1]))
            here = slice(g * rows, (g + 1) * rows)
            if t == 0:
                along = unit((start * ll) & (N_IMG - 1), N_IMG)
                along = (along[0][0:1] * scale1, along[1][0:1] * scale1)
                now = times((base[0], base[1]), along)
            else:
                now = (state[0, here], state[1, here])
            for part in range(parts):
                lanes = slice(t * depth + part * LANES, t * depth + (part + 1) * LANES)
                table[g * rows : (g + 1) * rows, lanes] = now[0].astype(BF16)
                table[S + g * rows : S + (g + 1) * rows, lanes] = now[1].astype(BF16)
                now = times(now, jump)
            if t + 1 < chunks:
                state[0, here], state[1, here] = now

    def finish(band):
        band[0] = (prod[:S, :cols] + prod[S:, cols:]).astype(BF16)
        band[1] = (prod[:S, cols:] - prod[S:, :cols]).astype(BF16)

    first_y = f * pixels + chip * SCOL * cols
    wide = 2 * N_IMG
    drow = 2 * iota((half, LANES), 0) + 1
    scale2 = 1.0 / math.sqrt(pixels * n_f)

    def fill_second():
        y = first_y + iota((half, LANES), 1)
        now = unit(product(drow, y, wide), wide)
        now = (now[0] * scale2, now[1] * scale2)
        jump = unit((drow * LANES) & (wide - 1), wide)
        for part in range(SCOL * cols // LANES):
            lanes = slice(part * LANES, (part + 1) * LANES)
            table2[:half, lanes] = now[0].astype(BF16)
            table2[half:, lanes] = now[1].astype(BF16)
            now = times(now, jump)
        for i in range(per):
            y = first_y + iota((8, SCOL * cols), 1)
            offset = 2 * soff_ref[core * per + i] + S - 1
            shift_tab[0, i], shift_tab[1, i] = unit(product(offset, y, wide), wide)

    idx[: 2 * blocks] = cell_ref[...]
    idx[2 * blocks :] = frac_ref[...]

    def to_reader(step):
        rf, rp = step // n_p, lax.rem(step, n_p)
        target = rp * SCOL + side
        return (rf, rp, target), pltpu.make_async_remote_copy(
            src_ref=idx,
            dst_ref=idx_all.at[lax.rem(f, per), c],
            send_sem=isend_sem.at[rf, rp],
            recv_sem=irecv_sem.at[lax.rem(f, per), c],
            device_id={"facet": rf, "col": target},
        )

    def away(facet, col):
        return jnp.logical_or(facet != f, col != c)

    def send_index(step):
        step = lax.rem(step + f * n_p + chip, n_f * n_p)
        (rf, rp, target), copy = to_reader(step)

        @pl.when(away(rf, target))
        def _():
            copy.start()

    mine = core
    other = 1 - core
    tables = (table_a, table_b)
    fill_table(table_a, other, 0)
    fill_second()
    for t in range(chunks):
        if t + 1 < chunks:
            fill_table(table_a, other, t + 1)
        else:
            for u in range(chunks):
                fill_table(table_b, mine, u)
        here = slice(t * depth, (t + 1) * depth)
        for index in range(2):
            loads[2 * t + index].wait()
            at = slice(index * cols, (index + 1) * cols)
            term = jnp.dot(table_a[:, here], sky[index, here], preferred_element_type=F32)
            if t == 0:
                prod[:, at] = term
            else:
                prod[:, at] += term
        if t == 0:
            pl.semaphore_wait(barrier, everyone - 1)
            each(n_f * n_p, send_index)

            @pl.when(side == core)
            def _():
                idx_all[lax.rem(f, per), c] = idx[...]

    finish(bsend)
    swap = pltpu.make_async_remote_copy(
        src_ref=bsend,
        dst_ref=bands.at[core],
        send_sem=band_sem.at[0],
        recv_sem=band_sem.at[1],
        device_id={"facet": f, "col": chip * SCOL + other},
    )
    swap.start()

    def index_from(step):
        i, cc = step // n_c, lax.rem(step, n_c)

        @pl.when(away(core * per + i, cc))
        def _():
            pltpu.make_async_remote_copy(
                src_ref=idx,
                dst_ref=idx_all.at[i, cc],
                send_sem=isend_sem.at[0, 0],
                recv_sem=irecv_sem.at[i, cc],
                device_id={"facet": core * per + i, "col": cc},
            ).wait_recv()

    each(per * n_c, index_from)

    sub = iota((8, slots), 0)

    def prepare(step):
        i, cc = step // n_c, lax.rem(step, n_c)
        block = idx_all[i, cc]
        cell, frac = block[: 2 * blocks], block[2 * blocks :]
        match = [frac == row for row in range(over)]
        taps = []
        for tap in range(ksize):
            value = jnp.zeros(frac.shape, F32)
            for row in range(over):
                value = jnp.where(match[row], kern_ref[tap, row], value)
            taps.append(value)
        low, high = cell & 7, cell >> 3

        def window(b, line):
            lo = low[b : b + 1]
            turn = (line - lo) & 7
            value = jnp.zeros((8, slots), F32)
            for tap in range(ksize):
                value = jnp.where(turn == tap, taps[tap][b : b + 1], value)
            return value, high[b : b + 1] + jnp.where(line < lo, 1, 0)

        for b in range(blocks):
            row_r[i, cc, b], row_t[i, cc, b] = window(b, sub)
            col_r[i, cc, b, 0], col_t[i, cc, b, 0] = window(blocks + b, sub)
            col_r[i, cc, b, 1], col_t[i, cc, b, 1] = window(blocks + b, 7 - sub)

    for index in range(2):
        at = slice(index * cols, (index + 1) * cols)
        prod[:, at] = jnp.dot(table_b[...], sky[index], preferred_element_type=F32)
    each(per * n_c, prepare)
    finish(bands.at[core])
    swap.wait_recv()

    def grid_of(i):
        for h in range(SCOL):
            at = slice(h * cols, (h + 1) * cols)
            sc = shift_tab[0, i, 0:1, at]
            sd = shift_tab[1, i, 0:1, at]
            re = bands[h, 0].astype(F32)
            im = bands[h, 1].astype(F32)
            stacked[:S, at] = (re * sc + im * sd).astype(BF16)
            stacked[S:, at] = (im * sc - re * sd).astype(BF16)
        both = lax.dot_general(
            table2[...], stacked[...], (((1,), (1,)), ((), ())), preferred_element_type=F32
        )
        even_re, even_im = both[:half, :S], both[:half, S:]
        odd_re, odd_im = both[half:, :S], both[half:, S:]
        cells[:half] = (even_re + odd_im).astype(BF16)
        cells[half:S] = (even_re - odd_im).astype(BF16)
        cells[S : S + half] = (even_im - odd_re).astype(BF16)
        cells[S + half :] = (even_im + odd_re).astype(BF16)

    def vis_copy(i, cc):
        return pltpu.make_async_remote_copy(
            src_ref=vsend.at[i, cc],
            dst_ref=vrecv.at[f, chip],
            send_sem=vsend_sem.at[i, cc],
            recv_sem=vrecv_sem.at[f, chip],
            device_id={"facet": core * per + i, "col": cc},
        )

    def degrid(i, cc, slot):
        for b in range(blocks):
            lanes = slice(b * slots, (b + 1) * slots)
            value, at = row_r[i, cc, b], row_t[i, cc, b]
            for g in range(S // 16):
                pair = [jnp.where(at == 2 * g + k, value, 0.0) for k in range(2)]
                weights[slot, 16 * g : 16 * (g + 1), lanes] = jnp.concatenate(pair, axis=0).astype(BF16)
        summed = jnp.dot(cells[...], weights[slot], preferred_element_type=F32)
        for b in range(blocks):
            lanes = slice(b * slots, (b + 1) * slots)
            zero = jnp.zeros((8, slots), F32)
            total_re, total_im = zero, zero
            for k in range(2):
                value, at = col_r[i, cc, b, k], col_t[i, cc, b, k]
                acc_re, acc_im = zero, zero
                for g in range(half // 8):
                    hit = at == (half // 8 + g if k == 0 else half // 8 - 1 - g)
                    top = k * half + 8 * g
                    acc_re = jnp.where(hit, summed[top : top + 8, lanes], acc_re)
                    acc_im = jnp.where(hit, summed[S + top : S + top + 8, lanes], acc_im)
                total_re = total_re + value * acc_re
                total_im = total_im + value * acc_im
            vsend[i, cc, b : b + 1] = jnp.sum(total_re, axis=0, keepdims=True)
            vsend[i, cc, blocks + b : blocks + b + 1] = jnp.sum(total_im, axis=0, keepdims=True)

        @pl.when(away(core * per + i, cc))
        def _():
            vis_copy(i, cc).start()

        @pl.when(jnp.logical_not(away(core * per + i, cc)))
        def _():
            vrecv[f, chip] = vsend[i, cc]

    flip = jnp.where(f < core * per + per // 2, 1, 0)
    for step in range(per):
        i = step + flip * (per - 1 - 2 * step)
        grid_of(i)

        def to_owner(turn, i=i):
            cc = exclusive(c, n_c - 1 - turn, n_c)
            degrid(i, cc, turn % 2)

        each(n_c, to_owner)

    def vis_from(step):
        sf, sp = step // n_p, lax.rem(step, n_p)

        @pl.when(away(sf, sp * SCOL + side))
        def _():
            pltpu.make_async_remote_copy(
                src_ref=vrecv.at[sf, sp],
                dst_ref=vrecv.at[sf, sp],
                send_sem=vsend_sem.at[0, 0],
                recv_sem=vrecv_sem.at[sf, sp],
                device_id={"facet": sf, "col": sp * SCOL + side},
            ).wait_recv()

    each(n_f * n_p, vis_from)
    acc = jnp.zeros((2 * blocks, slots), F32)
    for sf in range(n_f):
        for sp in range(n_p):
            acc = acc + vrecv[sf, sp]
    for b in range(blocks):
        live = iota((1, slots), 1) < count_ref[b]
        vis_ref[b : b + 1] = jnp.where(live, acc[b : b + 1], 0.0)
        vis_ref[blocks + b : blocks + b + 1] = jnp.where(live, acc[blocks + b : blocks + b + 1], 0.0)

    swap.wait_send()

    def index_sent(step):
        (rf, rp, target), copy = to_reader(step)

        @pl.when(away(rf, target))
        def _():
            copy.wait_send()

    def vis_sent(step):
        i, cc = step // n_c, lax.rem(step, n_c)

        @pl.when(away(core * per + i, cc))
        def _():
            vis_copy(i, cc).wait_send()

    each(n_f * n_p, index_sent)
    each(per * n_c, vis_sent)


def local(sky_re, sky_im, col_offsets, sub_offsets, kernel, vis_count, cell_index, frac_index):
    n_f = lax.axis_size("facet")
    n_c = lax.axis_size("col")
    pixels, cols = sky_re.shape[1:]
    subs = sub_offsets.shape[0]
    owned, blocks = vis_count.shape
    slots = cell_index.shape[-1]
    over, ksize = kernel.shape
    assert owned == 1 and subs == n_f
    chunks = 4
    per = subs // SCOL
    n_p = n_c // SCOL
    dims = (n_f, n_c, pixels, cols, subs, blocks, slots, chunks, ksize, over)
    smem = pl.BlockSpec(memory_space=pltpu.SMEM)
    vmem = pl.BlockSpec(memory_space=pltpu.VMEM)
    anywhere = pl.BlockSpec(memory_space=pl.ANY)
    dma = pltpu.SemaphoreType.DMA
    vis = pl.pallas_call(
        functools.partial(body, dims),
        out_shape=jax.ShapeDtypeStruct((2 * blocks, slots), F32),
        in_specs=[smem, smem, smem, smem, vmem, vmem, anywhere, anywhere],
        out_specs=vmem,
        scratch_shapes=[
            pltpu.VMEM((2, pixels, cols), BF16),
            pltpu.VMEM((2 * S, pixels), BF16),
            pltpu.VMEM((2 * S, pixels), BF16),
            pltpu.VMEM((2, S, LANES), F32),
            pltpu.VMEM((2 * S, 2 * cols), F32),
            pltpu.VMEM((4, 64, LANES), F32),
            pltpu.VMEM((2, per, 8, SCOL * cols), F32),
            pltpu.VMEM((S, SCOL * cols), BF16),
            pltpu.VMEM((2 * S, SCOL * cols), BF16),
            pltpu.VMEM((SCOL, 2, S, cols), BF16),
            pltpu.VMEM((2, S, cols), BF16),
            pltpu.VMEM((2 * S, S), BF16),
            pltpu.VMEM((4 * blocks, slots), jnp.int32),
            pltpu.VMEM((per, n_c, 4 * blocks, slots), jnp.int32),
            pltpu.VMEM((per, n_c, blocks, 8, slots), F32),
            pltpu.VMEM((per, n_c, blocks, 8, slots), jnp.int32),
            pltpu.VMEM((per, n_c, blocks, 2, 8, slots), F32),
            pltpu.VMEM((per, n_c, blocks, 2, 8, slots), jnp.int32),
            pltpu.VMEM((2, S, blocks * slots), BF16),
            pltpu.VMEM((per, n_c, 2 * blocks, slots), F32),
            pltpu.VMEM((n_f, n_p, 2 * blocks, slots), F32),
            dma((chunks, 2)),
            dma((2,)),
            dma((n_f, n_p)),
            dma((per, n_c)),
            dma((per, n_c)),
            dma((n_f, n_p)),
        ],
        compiler_params=pltpu.CompilerParams(
            collective_id=0, has_side_effects=True, vmem_limit_bytes=60 << 20
        ),
    )(
        col_offsets,
        sub_offsets,
        kernel.T,
        vis_count.reshape(blocks),
        cell_index.reshape(2 * blocks, slots),
        frac_index.reshape(2 * blocks, slots),
        sky_re,
        sky_im,
    )
    vis = vis.reshape(2, 1, blocks, slots)
    return (vis[0], vis[1])


def solution(mesh):
    placed = (
        P("facet", None, "col"),
        P("facet", None, "col"),
        P(),
        P(),
        P(),
        P("facet", "col"),
        P(None, "facet", "col", None),
        P(None, "facet", "col", None),
    )
    return jax.shard_map(
        local,
        mesh=mesh,
        in_specs=placed,
        out_specs=(P("facet", "col", None), P("facet", "col", None)),
        check_vma=False,
    )
```

time: 35.7 us -> 31.2 us (0.87)
  Pallas kernels: 33.5 us -> 29 us
    pallas_call x1, Pallas kernels: 33.5 us -> 29 us  [local(): pl.pallas_call(functools.partial(body, dims), out_shape=jax.ShapeDtypeStr...]
where the time goes in v1:
time: 31.2 us; the launch traced here: 31 us
  Pallas kernels  29 us (93%)
  local copies, waits for them, and re-layouts  1.33 us (4%)
  between operations  0.64 us (2%)
    pallas_call x1, Pallas kernels, local(): pl.pallas_call(functools.partial(body, dims), out_shape=jax.ShapeDtypeStr...  29 us
    squeeze x1, local copies, waits for them, and re-layouts, local(): return (vis[0], vis[1])  1.33 us

profile of v1, /device:TPU:0, one launch (start us, length us, event | category | flops | bytes accessed | tf_op | source)
XLA Modules:
  0.0 31.0 jit_solution(5345090213139445067)
XLA Ops:
  0.6 29.0 %shard_map.95 = f32[8,128]{1,0:T(8,128)} custom-call(s32[2]{0:T(128)} %coff_ref.1, s32[4]{0:T(128)} %soff_ref.1, f32[8,16]{1,0:T(8,128)} %bitcast.8, s32[4]{0:T(128)} %bitcast.11, s32[8,128]{1,0:T(8,128)} %bitcast.9, s32[8,128]{1,0:T(8,128)} %bitcast.10, bf16[1,4096,512]{2,1,0:T(8,128)(2,1)} %re_hbm.1, bf16[1,4096,512]{2,1,0:T(8,128)(2,1)} %im_hbm.1), custom_call_target="tpu_custom_call" | custom-call | tf_op jit(solution)/shard_map/pallas_call | solution.py:447
  29.6 1.3 %slice_bitcast_fusion = (f32[1,4,128]{2,1,0:T(4,128)}, f32[1,4,128]{2,1,0:T(4,128)}) fusion(f32[8,128]{1,0:T(8,128)} %shard_map.95), kind=kLoop, calls=%fused_computation | loop fusion | bytes 8192 | tf_op jit(solution)/shard_map/squeeze | solution.py:495

commit v2 on v1

--- a/solution.py
+++ b/solution.py
@@ -99,10 +99,6 @@
     cells,
     idx,
     idx_all,
-    row_r,
-    row_t,
-    col_r,
-    col_t,
     weights,
     vsend,
     vrecv,
@@ -116,7 +112,6 @@
     n_f, n_c, pixels, cols, subs, blocks, slots, chunks, ksize, over = dims
     per = subs // SCOL
     n_p = n_c // SCOL
-    half = S // 2
     rows = 64
     f = lax.axis_index("facet")
     c = lax.axis_index("col")
@@ -180,49 +175,58 @@
         band[1] = (prod[:S, cols:] - prod[S:, :cols]).astype(BF16)
 
     first_y = f * pixels + chip * SCOL * cols
-    wide = 2 * N_IMG
-    drow = 2 * iota((half, LANES), 0) + 1
     scale2 = 1.0 / math.sqrt(pixels * n_f)
 
     def fill_second():
-        y = first_y + iota((half, LANES), 1)
-        now = unit(product(drow, y, wide), wide)
-        now = (now[0] * scale2, now[1] * scale2)
-        jump = unit((drow * LANES) & (wide - 1), wide)
-        for part in range(SCOL * cols // LANES):
-            lanes = slice(part * LANES, (part + 1) * LANES)
-            table2[:half, lanes] = now[0].astype(BF16)
-            table2[half:, lanes] = now[1].astype(BF16)
-            now = times(now, jump)
+        for g in range(S // rows):
+            k = iota((rows, LANES), 0) + g * rows
+            y = first_y + iota((rows, LANES), 1)
+            now = unit(product(k, y, N_IMG), N_IMG)
+            now = (now[0] * scale2, now[1] * scale2)
+            jump = unit((k * LANES) & (N_IMG - 1), N_IMG)
+            for part in range(SCOL * cols // LANES):
+                lanes = slice(part * LANES, (part + 1) * LANES)
+                table2[g * rows : (g + 1) * rows, lanes] = now[0].astype(BF16)
+                table2[S + g * rows : S + (g + 1) * rows, lanes] = now[1].astype(BF16)
+                now = times(now, jump)
         for i in range(per):
             y = first_y + iota((8, SCOL * cols), 1)
-            offset = 2 * soff_ref[core * per + i] + S - 1
-            shift_tab[0, i], shift_tab[1, i] = unit(product(offset, y, wide), wide)
+            shift_tab[0, i], shift_tab[1, i] = unit(product(soff_ref[core * per + i], y, N_IMG), N_IMG)
 
     idx[: 2 * blocks] = cell_ref[...]
     idx[2 * blocks :] = frac_ref[...]
 
+    def away(facet, col):
+        return jnp.logical_or(facet != f, col != c)
+
+    own_index = idx_all.at[lax.rem(f, per), c]
+    own_sem = irecv_sem.at[lax.rem(f, per), c]
+
     def to_reader(step):
-        rf, rp = step // n_p, lax.rem(step, n_p)
+        rf = lax.rem(f + step // n_p, n_f)
+        rp = lax.rem(chip + lax.rem(step, n_p), n_p)
         target = rp * SCOL + side
-        return (rf, rp, target), pltpu.make_async_remote_copy(
+        return (rf, target), pltpu.make_async_remote_copy(
             src_ref=idx,
-            dst_ref=idx_all.at[lax.rem(f, per), c],
+            dst_ref=own_index,
             send_sem=isend_sem.at[rf, rp],
-            recv_sem=irecv_sem.at[lax.rem(f, per), c],
+            recv_sem=own_sem,
             device_id={"facet": rf, "col": target},
         )
 
-    def away(facet, col):
-        return jnp.logical_or(facet != f, col != c)
-
     def send_index(step):
-        step = lax.rem(step + f * n_p + chip, n_f * n_p)
-        (rf, rp, target), copy = to_reader(step)
+        (rf, target), copy = to_reader(step)
+        if isinstance(step, int) and step > 0:
+            copy.start()
+            return
 
         @pl.when(away(rf, target))
         def _():
             copy.start()
+
+        @pl.when(jnp.logical_not(away(rf, target)))
+        def _():
+            pltpu.make_async_copy(idx, own_index, own_sem).start()
 
     mine = core
     other = 1 - core
@@ -244,14 +248,6 @@
                 prod[:, at] = term
             else:
                 prod[:, at] += term
-        if t == 0:
-            pl.semaphore_wait(barrier, everyone - 1)
-            each(n_f * n_p, send_index)
-
-            @pl.when(side == core)
-            def _():
-                idx_all[lax.rem(f, per), c] = idx[...]
-
     finish(bsend)
     swap = pltpu.make_async_remote_copy(
         src_ref=bsend,
@@ -260,27 +256,15 @@
         recv_sem=band_sem.at[1],
         device_id={"facet": f, "col": chip * SCOL + other},
     )
-    swap.start()
-
-    def index_from(step):
-        i, cc = step // n_c, lax.rem(step, n_c)
-
-        @pl.when(away(core * per + i, cc))
-        def _():
-            pltpu.make_async_remote_copy(
-                src_ref=idx,
-                dst_ref=idx_all.at[i, cc],
-                send_sem=isend_sem.at[0, 0],
-                recv_sem=irecv_sem.at[i, cc],
-                device_id={"facet": core * per + i, "col": cc},
-            ).wait_recv()
-
-    each(per * n_c, index_from)
+
+    def index_from(i, cc):
+        pltpu.make_async_copy(idx, idx_all.at[i, cc], irecv_sem.at[i, cc]).wait()
 
     sub = iota((8, slots), 0)
 
-    def prepare(step):
-        i, cc = step // n_c, lax.rem(step, n_c)
+    sub16 = iota((16, slots), 0)
+
+    def prepare(i, cc):
         block = idx_all[i, cc]
         cell, frac = block[: 2 * blocks], block[2 * blocks :]
         match = [frac == row for row in range(over)]
@@ -290,25 +274,26 @@
             for row in range(over):
                 value = jnp.where(match[row], kern_ref[tap, row], value)
             taps.append(value)
-        low, high = cell & 7, cell >> 3
 
         def window(b, line):
-            lo = low[b : b + 1]
-            turn = (line - lo) & 7
-            value = jnp.zeros((8, slots), F32)
+            size = line.shape[0]
+            lo = cell[b : b + 1] & (size - 1)
+            turn = (line - lo) & (size - 1)
+            value = jnp.zeros(line.shape, F32)
             for tap in range(ksize):
                 value = jnp.where(turn == tap, taps[tap][b : b + 1], value)
-            return value, high[b : b + 1] + jnp.where(line < lo, 1, 0)
-
-        for b in range(blocks):
-            row_r[i, cc, b], row_t[i, cc, b] = window(b, sub)
-            col_r[i, cc, b, 0], col_t[i, cc, b, 0] = window(blocks + b, sub)
-            col_r[i, cc, b, 1], col_t[i, cc, b, 1] = window(blocks + b, 7 - sub)
+            high = cell[b : b + 1] >> (size.bit_length() - 1)
+            return value, high + jnp.where(line < lo, 1, 0)
+
+        return [window(b, sub16) for b in range(blocks)], [window(blocks + b, sub) for b in range(blocks)]
 
     for index in range(2):
         at = slice(index * cols, (index + 1) * cols)
         prod[:, at] = jnp.dot(table_b[...], sky[index], preferred_element_type=F32)
-    each(per * n_c, prepare)
+        if index == 0:
+            pl.semaphore_wait(barrier, everyone - 1)
+            swap.start()
+            each(n_f * n_p, send_index)
     finish(bands.at[core])
     swap.wait_recv()
 
@@ -324,12 +309,10 @@
         both = lax.dot_general(
             table2[...], stacked[...], (((1,), (1,)), ((), ())), preferred_element_type=F32
         )
-        even_re, even_im = both[:half, :S], both[:half, S:]
-        odd_re, odd_im = both[half:, :S], both[half:, S:]
-        cells[:half] = (even_re + odd_im).astype(BF16)
-        cells[half:S] = (even_re - odd_im).astype(BF16)
-        cells[S : S + half] = (even_im - odd_re).astype(BF16)
-        cells[S + half :] = (even_im + odd_re).astype(BF16)
+        cells[i, :S] = (both[:S, :S] + both[S:, S:]).astype(BF16)
+        cells[i, S:] = (both[:S, S:] - both[S:, :S]).astype(BF16)
+
+    each(per, grid_of)
 
     def vis_copy(i, cc):
         return pltpu.make_async_remote_copy(
@@ -341,29 +324,30 @@
         )
 
     def degrid(i, cc, slot):
+        row, col = prepare(i, cc)
         for b in range(blocks):
             lanes = slice(b * slots, (b + 1) * slots)
-            value, at = row_r[i, cc, b], row_t[i, cc, b]
+            value, at = row[b][0].astype(BF16), row[b][1].astype(jnp.int16)
             for g in range(S // 16):
-                pair = [jnp.where(at == 2 * g + k, value, 0.0) for k in range(2)]
-                weights[slot, 16 * g : 16 * (g + 1), lanes] = jnp.concatenate(pair, axis=0).astype(BF16)
-        summed = jnp.dot(cells[...], weights[slot], preferred_element_type=F32)
+                weights[slot, 16 * g : 16 * (g + 1), lanes] = jnp.where(
+                    at == jnp.int16(g), value, jnp.zeros_like(value)
+                )
+        summed = jnp.dot(cells[i], weights[slot], preferred_element_type=F32)
         for b in range(blocks):
             lanes = slice(b * slots, (b + 1) * slots)
-            zero = jnp.zeros((8, slots), F32)
-            total_re, total_im = zero, zero
-            for k in range(2):
-                value, at = col_r[i, cc, b, k], col_t[i, cc, b, k]
-                acc_re, acc_im = zero, zero
-                for g in range(half // 8):
-                    hit = at == (half // 8 + g if k == 0 else half // 8 - 1 - g)
-                    top = k * half + 8 * g
-                    acc_re = jnp.where(hit, summed[top : top + 8, lanes], acc_re)
-                    acc_im = jnp.where(hit, summed[S + top : S + top + 8, lanes], acc_im)
-                total_re = total_re + value * acc_re
-                total_im = total_im + value * acc_im
-            vsend[i, cc, b : b + 1] = jnp.sum(total_re, axis=0, keepdims=True)
-            vsend[i, cc, blocks + b : blocks + b + 1] = jnp.sum(total_im, axis=0, keepdims=True)
+            value, at = col[b]
+            acc_re = acc_im = jnp.zeros((8, slots), F32)
+            for g in range(S // 8):
+                hit = at == g
+                acc_re = jnp.where(hit, summed[8 * g : 8 * g + 8, lanes], acc_re)
+                acc_im = jnp.where(hit, summed[S + 8 * g : S + 8 * g + 8, lanes], acc_im)
+            vsend[i, cc, b : b + 1] = jnp.sum(value * acc_re, axis=0, keepdims=True)
+            vsend[i, cc, blocks + b : blocks + b + 1] = jnp.sum(value * acc_im, axis=0, keepdims=True)
+
+    def send_vis(i, cc, near):
+        if not near:
+            vis_copy(i, cc).start()
+            return
 
         @pl.when(away(core * per + i, cc))
         def _():
@@ -371,31 +355,31 @@
 
         @pl.when(jnp.logical_not(away(core * per + i, cc)))
         def _():
-            vrecv[f, chip] = vsend[i, cc]
+            pltpu.make_async_copy(vsend.at[i, cc], vrecv.at[f, chip], vrecv_sem.at[f, chip]).start()
 
     flip = jnp.where(f < core * per + per // 2, 1, 0)
+    batch = min(n_c, 4)
     for step in range(per):
         i = step + flip * (per - 1 - 2 * step)
-        grid_of(i)
-
-        def to_owner(turn, i=i):
-            cc = exclusive(c, n_c - 1 - turn, n_c)
-            degrid(i, cc, turn % 2)
-
-        each(n_c, to_owner)
+
+        def arrive(cc, i=i):
+            index_from(i, cc)
+
+        each(n_c, arrive)
+
+        def to_owners(turn, i=i):
+            owners = [exclusive(c, n_c - 1 - turn * batch - k, n_c) for k in range(batch)]
+            for k, cc in enumerate(owners):
+                degrid(i, cc, k)
+            for k, cc in enumerate(owners):
+                last = k == batch - 1
+                send_vis(i, cc, last if not isinstance(turn, int) else last and turn == n_c // batch - 1)
+
+        each(n_c // batch, to_owners)
 
     def vis_from(step):
         sf, sp = step // n_p, lax.rem(step, n_p)
-
-        @pl.when(away(sf, sp * SCOL + side))
-        def _():
-            pltpu.make_async_remote_copy(
-                src_ref=vrecv.at[sf, sp],
-                dst_ref=vrecv.at[sf, sp],
-                send_sem=vsend_sem.at[0, 0],
-                recv_sem=vrecv_sem.at[sf, sp],
-                device_id={"facet": sf, "col": sp * SCOL + side},
-            ).wait_recv()
+        pltpu.make_async_copy(vsend.at[0, 0], vrecv.at[sf, sp], vrecv_sem.at[sf, sp]).wait()
 
     each(n_f * n_p, vis_from)
     acc = jnp.zeros((2 * blocks, slots), F32)
@@ -410,14 +394,20 @@
     swap.wait_send()
 
     def index_sent(step):
-        (rf, rp, target), copy = to_reader(step)
+        (rf, target), copy = to_reader(step)
+        if isinstance(step, int) and step > 0:
+            copy.wait_send()
+            return
 
         @pl.when(away(rf, target))
         def _():
             copy.wait_send()
 
     def vis_sent(step):
-        i, cc = step // n_c, lax.rem(step, n_c)
+        i, cc = lax.rem(step, per), lax.rem(c + step // per, n_c)
+        if isinstance(step, int) and step >= per:
+            vis_copy(i, cc).wait_send()
+            return
 
         @pl.when(away(core * per + i, cc))
         def _():
@@ -457,18 +447,14 @@
             pltpu.VMEM((2 * S, 2 * cols), F32),
             pltpu.VMEM((4, 64, LANES), F32),
             pltpu.VMEM((2, per, 8, SCOL * cols), F32),
-            pltpu.VMEM((S, SCOL * cols), BF16),
+            pltpu.VMEM((2 * S, SCOL * cols), BF16),
             pltpu.VMEM((2 * S, SCOL * cols), BF16),
             pltpu.VMEM((SCOL, 2, S, cols), BF16),
             pltpu.VMEM((2, S, cols), BF16),
-            pltpu.VMEM((2 * S, S), BF16),
+            pltpu.VMEM((per, 2 * S, S), BF16),
             pltpu.VMEM((4 * blocks, slots), jnp.int32),
             pltpu.VMEM((per, n_c, 4 * blocks, slots), jnp.int32),
-            pltpu.VMEM((per, n_c, blocks, 8, slots), F32),
-            pltpu.VMEM((per, n_c, blocks, 8, slots), jnp.int32),
-            pltpu.VMEM((per, n_c, blocks, 2, 8, slots), F32),
-            pltpu.VMEM((per, n_c, blocks, 2, 8, slots), jnp.int32),
-            pltpu.VMEM((2, S, blocks * slots), BF16),
+            pltpu.VMEM((min(n_c, 4), S, blocks * slots), BF16),
             pltpu.VMEM((per, n_c, 2 * blocks, slots), F32),
             pltpu.VMEM((n_f, n_p, 2 * blocks, slots), F32),
             dma((chunks, 2)),

time: 31.2 us -> 29.4 us (0.942)
  Pallas kernels: 29 us -> 27.2 us
    pallas_call x1, Pallas kernels: 29 us -> 27.2 us  [local(): pl.pallas_call(functools.partial(body, dims), out_shape=jax.ShapeDtypeStr...]
where the time goes in v2:
time: 29.4 us; the launch traced here: 29.1 us
  Pallas kernels  27.2 us (93%)
  local copies, waits for them, and re-layouts  1.33 us (5%)
  between operations  0.64 us (2%)
    pallas_call x1, Pallas kernels, local(): pl.pallas_call(functools.partial(body, dims), out_shape=jax.ShapeDtypeStr...  27.2 us
    squeeze x1, local copies, waits for them, and re-layouts, local(): return (vis[0], vis[1])  1.33 us

profile of v2, /device:TPU:0, one launch (start us, length us, event | category | flops | bytes accessed | tf_op | source)
XLA Modules:
  0.0 29.1 jit_solution(3932273008703880677)
XLA Ops:
  0.6 27.2 %shard_map.95 = f32[8,128]{1,0:T(8,128)} custom-call(s32[2]{0:T(128)} %coff_ref.1, s32[4]{0:T(128)} %soff_ref.1, f32[8,16]{1,0:T(8,128)} %bitcast.8, s32[4]{0:T(128)} %bitcast.11, s32[8,128]{1,0:T(8,128)} %bitcast.9, s32[8,128]{1,0:T(8,128)} %bitcast.10, bf16[1,4096,512]{2,1,0:T(8,128)(2,1)} %re_hbm.1, bf16[1,4096,512]{2,1,0:T(8,128)(2,1)} %im_hbm.1), custom_call_target="tpu_custom_call" | custom-call | tf_op jit(solution)/shard_map/pallas_call | solution.py:437
  27.8 1.3 %slice_bitcast_fusion = (f32[1,4,128]{2,1,0:T(4,128)}, f32[1,4,128]{2,1,0:T(4,128)}) fusion(f32[8,128]{1,0:T(8,128)} %shard_map.95), kind=kLoop, calls=%fused_computation | loop fusion | bytes 8192 | tf_op jit(solution)/shard_map/squeeze | solution.py:481

commit v3 on v2

--- a/solution.py
+++ b/solution.py
@@ -86,12 +86,14 @@
     im_hbm,
     vis_ref,
     sky,
-    table_a,
-    table_b,
+    folded,
+    table,
+    flip_mat,
     state,
     prod,
     base,
     shift_tab,
+    turn_tab,
     table2,
     stacked,
     bands,
@@ -118,18 +120,20 @@
     core = lax.rem(c, SCOL)
     chip = c // SCOL
     side = f // per
-    depth = pixels // chunks
+    depth = pixels // 2 // chunks
+    wide = 2 * N_IMG
 
     loads = []
     for t in range(chunks):
-        for index, src in enumerate((re_hbm, im_hbm)):
-            copy = pltpu.make_async_copy(
-                src.at[0, pl.ds(t * depth, depth)],
-                sky.at[index, pl.ds(t * depth, depth)],
-                sky_sem.at[t, index],
-            )
-            copy.start()
-            loads.append(copy)
+        for k, start in enumerate((t * depth, pixels - (t + 1) * depth)):
+            for index, src in enumerate((re_hbm, im_hbm)):
+                copy = pltpu.make_async_copy(
+                    src.at[0, pl.ds(start, depth)],
+                    sky.at[index, pl.ds(start, depth)],
+                    sky_sem.at[t, 2 * k + index],
+                )
+                copy.start()
+                loads.append(copy)
 
     barrier = pltpu.get_barrier_semaphore()
     everyone = n_f * n_c
@@ -143,36 +147,57 @@
     each(everyone - 1, greet)
 
     jrow = iota((rows, LANES), 0)
-    lane = iota((rows, LANES), 1)
-    base[0], base[1] = unit(jrow * lane, N_IMG)
-    base[2], base[3] = unit(jrow * LANES, N_IMG)
+    twice = pixels - 1 - 2 * iota((rows, LANES), 1)
+    base[0], base[1] = unit((jrow * twice) & (wide - 1), wide)
+    base[2], base[3] = unit((jrow * (2 * LANES)) & (wide - 1), wide)
     scale1 = 1.0 / math.sqrt(pixels)
-
-    def fill_table(table, q, t):
-        parts = depth // LANES
-        for g in range(S // rows):
-            start = coff_ref[q] + g * rows
-            ll = iota((8, LANES), 1)
-            jump = unit((start * LANES + 0 * ll) & (N_IMG - 1), N_IMG)
-            jump = times((base[2], base[3]), (jump[0][0:1], jump[1][0:1]))
-            here = slice(g * rows, (g + 1) * rows)
-            if t == 0:
-                along = unit((start * ll) & (N_IMG - 1), N_IMG)
-                along = (along[0][0:1] * scale1, along[1][0:1] * scale1)
-                now = times((base[0], base[1]), along)
-            else:
-                now = (state[0, here], state[1, here])
-            for part in range(parts):
-                lanes = slice(t * depth + part * LANES, t * depth + (part + 1) * LANES)
-                table[g * rows : (g + 1) * rows, lanes] = now[0].astype(BF16)
-                table[S + g * rows : S + (g + 1) * rows, lanes] = now[1].astype(BF16)
-                now = times(now, jump)
-            if t + 1 < chunks:
-                state[0, here], state[1, here] = now
-
-    def finish(band):
-        band[0] = (prod[:S, :cols] + prod[S:, cols:]).astype(BF16)
-        band[1] = (prod[:S, cols:] - prod[S:, :cols]).astype(BF16)
+    order = (1 - core, core)
+
+    def fill_table(t):
+        for n, q in enumerate(order):
+            for g in range(S // rows):
+                start = coff_ref[q] + g * rows
+                ll = pixels - 1 - 2 * iota((8, LANES), 1)
+                jump = unit((start * (2 * LANES) + 0 * ll) & (wide - 1), wide)
+                jump = times((base[2], base[3]), (jump[0][0:1], jump[1][0:1]))
+                jump = (jump[0], -jump[1])
+                here = slice(n * S + g * rows, n * S + (g + 1) * rows)
+                if t == 0:
+                    along = unit((start * ll) & (wide - 1), wide)
+                    along = (along[0][0:1] * scale1, along[1][0:1] * scale1)
+                    now = times((base[0], base[1]), along)
+                else:
+                    now = (state[0, here], state[1, here])
+                for part in range(depth // LANES):
+                    lanes = slice(2 * t * depth + part * LANES, 2 * t * depth + (part + 1) * LANES)
+                    table[here, lanes] = now[0].astype(BF16)
+                    lanes = slice(lanes.start + depth, lanes.stop + depth)
+                    table[here, lanes] = now[1].astype(BF16)
+                    now = times(now, jump)
+                if t + 1 < chunks:
+                    state[0, here], state[1, here] = now
+
+    tile = flip_mat.shape[0]
+    flip_mat[...] = jnp.where(iota((tile, tile), 0) + iota((tile, tile), 1) == tile - 1, 1.0, 0.0).astype(BF16)
+
+    def fold(t):
+        for index in range(2):
+            loads[4 * t + index].wait()
+            loads[4 * t + 2 + index].wait()
+            here = slice(index * cols, (index + 1) * cols)
+            there = slice((1 - index) * cols, (2 - index) * cols)
+            for k in range(0, depth, tile):
+                high = sky[index, pixels - t * depth - k - tile : pixels - t * depth - k]
+                high = jnp.dot(flip_mat[...], high, preferred_element_type=F32).astype(BF16)
+                low = sky[index, t * depth + k : t * depth + k + tile]
+                top = 2 * t * depth + k
+                folded[top : top + tile, here] = low + high
+                top = top + depth
+                folded[top : top + tile, there] = low - high if index == 0 else high - low
+
+    def finish(band, top):
+        for index in range(2):
+            band[index] = prod[top : top + S, index * cols : (index + 1) * cols].astype(BF16)
 
     first_y = f * pixels + chip * SCOL * cols
     scale2 = 1.0 / math.sqrt(pixels * n_f)
@@ -193,6 +218,9 @@
             y = first_y + iota((8, SCOL * cols), 1)
             shift_tab[0, i], shift_tab[1, i] = unit(product(soff_ref[core * per + i], y, N_IMG), N_IMG)
 
+        j = coff_ref[core] + iota((8, S), 1)
+        turn_tab[0], turn_tab[1] = unit((j * (pixels - 1)) & (wide - 1), wide)
+
     idx[: 2 * blocks] = cell_ref[...]
     idx[2 * blocks :] = frac_ref[...]
 
@@ -228,27 +256,24 @@
         def _():
             pltpu.make_async_copy(idx, own_index, own_sem).start()
 
-    mine = core
     other = 1 - core
-    tables = (table_a, table_b)
-    fill_table(table_a, other, 0)
+    fill_table(0)
+    fold(0)
     fill_second()
     for t in range(chunks):
         if t + 1 < chunks:
-            fill_table(table_a, other, t + 1)
-        else:
-            for u in range(chunks):
-                fill_table(table_b, mine, u)
-        here = slice(t * depth, (t + 1) * depth)
+            fill_table(t + 1)
+            fold(t + 1)
+        here = slice(2 * t * depth, 2 * (t + 1) * depth)
         for index in range(2):
-            loads[2 * t + index].wait()
             at = slice(index * cols, (index + 1) * cols)
-            term = jnp.dot(table_a[:, here], sky[index, here], preferred_element_type=F32)
+            term = jnp.dot(table[:, here], folded[here, at], preferred_element_type=F32)
             if t == 0:
                 prod[:, at] = term
             else:
                 prod[:, at] += term
-    finish(bsend)
+
+    finish(bsend, 0)
     swap = pltpu.make_async_remote_copy(
         src_ref=bsend,
         dst_ref=bands.at[core],
@@ -256,6 +281,10 @@
         recv_sem=band_sem.at[1],
         device_id={"facet": f, "col": chip * SCOL + other},
     )
+
+    pl.semaphore_wait(barrier, everyone - 1)
+    swap.start()
+    each(n_f * n_p, send_index)
 
     def index_from(i, cc):
         pltpu.make_async_copy(idx, idx_all.at[i, cc], irecv_sem.at[i, cc]).wait()
@@ -287,14 +316,7 @@
 
         return [window(b, sub16) for b in range(blocks)], [window(blocks + b, sub) for b in range(blocks)]
 
-    for index in range(2):
-        at = slice(index * cols, (index + 1) * cols)
-        prod[:, at] = jnp.dot(table_b[...], sky[index], preferred_element_type=F32)
-        if index == 0:
-            pl.semaphore_wait(barrier, everyone - 1)
-            swap.start()
-            each(n_f * n_p, send_index)
-    finish(bands.at[core])
+    finish(bands.at[core], S)
     swap.wait_recv()
 
     def grid_of(i):
@@ -309,8 +331,11 @@
         both = lax.dot_general(
             table2[...], stacked[...], (((1,), (1,)), ((), ())), preferred_element_type=F32
         )
-        cells[i, :S] = (both[:S, :S] + both[S:, S:]).astype(BF16)
-        cells[i, S:] = (both[:S, S:] - both[S:, :S]).astype(BF16)
+        re = both[:S, :S] + both[S:, S:]
+        im = both[:S, S:] - both[S:, :S]
+        tc, td = turn_tab[0, 0:1], turn_tab[1, 0:1]
+        cells[i, :S] = (re * tc + im * td).astype(BF16)
+        cells[i, S:] = (im * tc - re * td).astype(BF16)
 
     each(per, grid_of)
 
@@ -441,12 +466,14 @@
         out_specs=vmem,
         scratch_shapes=[
             pltpu.VMEM((2, pixels, cols), BF16),
+            pltpu.VMEM((pixels, 2 * cols), BF16),
             pltpu.VMEM((2 * S, pixels), BF16),
-            pltpu.VMEM((2 * S, pixels), BF16),
-            pltpu.VMEM((2, S, LANES), F32),
+            pltpu.VMEM((256, 256), BF16),
+            pltpu.VMEM((2, 2 * S, LANES), F32),
             pltpu.VMEM((2 * S, 2 * cols), F32),
             pltpu.VMEM((4, 64, LANES), F32),
             pltpu.VMEM((2, per, 8, SCOL * cols), F32),
+            pltpu.VMEM((2, 8, S), F32),
             pltpu.VMEM((2 * S, SCOL * cols), BF16),
             pltpu.VMEM((2 * S, SCOL * cols), BF16),
             pltpu.VMEM((SCOL, 2, S, cols), BF16),
@@ -457,7 +484,7 @@
             pltpu.VMEM((min(n_c, 4), S, blocks * slots), BF16),
             pltpu.VMEM((per, n_c, 2 * blocks, slots), F32),
             pltpu.VMEM((n_f, n_p, 2 * blocks, slots), F32),
-            dma((chunks, 2)),
+            dma((chunks, 4)),
             dma((2,)),
             dma((n_f, n_p)),
             dma((per, n_c)),

time: 29.4 us -> 28.1 us (0.956)
  Pallas kernels: 27.2 us -> 25.9 us
    pallas_call x1, Pallas kernels: 27.2 us -> 25.9 us  [local(): pl.pallas_call(functools.partial(body, dims), out_shape=jax.ShapeDtypeStr...]
where the time goes in v3:
time: 28.1 us; the launch traced here: 27.9 us
  Pallas kernels  25.9 us (92%)
  local copies, waits for them, and re-layouts  1.33 us (5%)
  between operations  0.64 us (2%)
    pallas_call x1, Pallas kernels, local(): pl.pallas_call(functools.partial(body, dims), out_shape=jax.ShapeDtypeStr...  25.9 us
    squeeze x1, local copies, waits for them, and re-layouts, local(): return (vis[0], vis[1])  1.33 us

profile of v3, /device:TPU:0, one launch (start us, length us, event | category | flops | bytes accessed | tf_op | source)
XLA Modules:
  0.0 27.9 jit_solution(9820861359178183600)
XLA Ops:
  0.6 25.9 %shard_map.95 = f32[8,128]{1,0:T(8,128)} custom-call(s32[2]{0:T(128)} %coff_ref.1, s32[4]{0:T(128)} %soff_ref.1, f32[8,16]{1,0:T(8,128)} %bitcast.8, s32[4]{0:T(128)} %bitcast.11, s32[8,128]{1,0:T(8,128)} %bitcast.9, s32[8,128]{1,0:T(8,128)} %bitcast.10, bf16[1,4096,512]{2,1,0:T(8,128)(2,1)} %re_hbm.1, bf16[1,4096,512]{2,1,0:T(8,128)(2,1)} %im_hbm.1), custom_call_target="tpu_custom_call" | custom-call | tf_op jit(solution)/shard_map/pallas_call | solution.py:462
  26.6 1.3 %slice_bitcast_fusion = (f32[1,4,128]{2,1,0:T(4,128)}, f32[1,4,128]{2,1,0:T(4,128)}) fusion(f32[8,128]{1,0:T(8,128)} %shard_map.95), kind=kLoop, calls=%fused_computation | loop fusion | bytes 8192 | tf_op jit(solution)/shard_map/squeeze | solution.py:508

commit v4 on v3

--- a/solution.py
+++ b/solution.py
@@ -182,8 +182,6 @@
 
     def fold(t):
         for index in range(2):
-            loads[4 * t + index].wait()
-            loads[4 * t + 2 + index].wait()
             here = slice(index * cols, (index + 1) * cols)
             there = slice((1 - index) * cols, (2 - index) * cols)
             for k in range(0, depth, tile):
@@ -203,26 +201,29 @@
     scale2 = 1.0 / math.sqrt(pixels * n_f)
 
     def fill_second():
-        for g in range(S // rows):
-            k = iota((rows, LANES), 0) + g * rows
-            y = first_y + iota((rows, LANES), 1)
-            now = unit(product(k, y, N_IMG), N_IMG)
-            now = (now[0] * scale2, now[1] * scale2)
-            jump = unit((k * LANES) & (N_IMG - 1), N_IMG)
-            for part in range(SCOL * cols // LANES):
-                lanes = slice(part * LANES, (part + 1) * LANES)
-                table2[g * rows : (g + 1) * rows, lanes] = now[0].astype(BF16)
-                table2[S + g * rows : S + (g + 1) * rows, lanes] = now[1].astype(BF16)
-                now = times(now, jump)
-        for i in range(per):
-            y = first_y + iota((8, SCOL * cols), 1)
-            shift_tab[0, i], shift_tab[1, i] = unit(product(soff_ref[core * per + i], y, N_IMG), N_IMG)
-
+        for h, place in enumerate((core, 1 - core)):
+            begin = first_y + place * cols
+            for g in range(S // rows):
+                k = iota((rows, LANES), 0) + g * rows
+                y = begin + iota((rows, LANES), 1)
+                now = unit(product(k, y, N_IMG), N_IMG)
+                now = (now[0] * scale2, now[1] * scale2)
+                jump = unit((k * LANES) & (N_IMG - 1), N_IMG)
+                for part in range(cols // LANES):
+                    lanes = slice(h * cols + part * LANES, h * cols + (part + 1) * LANES)
+                    table2[g * rows : (g + 1) * rows, lanes] = now[0].astype(BF16)
+                    table2[S + g * rows : S + (g + 1) * rows, lanes] = now[1].astype(BF16)
+                    now = times(now, jump)
+            for i in range(per):
+                at = slice(h * cols, (h + 1) * cols)
+                y = begin + iota((8, cols), 1)
+                turn = unit(product(soff_ref[core * per + i], y, N_IMG), N_IMG)
+                shift_tab[0, i, :, at], shift_tab[1, i, :, at] = turn
         j = coff_ref[core] + iota((8, S), 1)
         turn_tab[0], turn_tab[1] = unit((j * (pixels - 1)) & (wide - 1), wide)
 
-    idx[: 2 * blocks] = cell_ref[...]
-    idx[2 * blocks :] = frac_ref[...]
+    both_index = jnp.concatenate([cell_ref[...], frac_ref[...]], axis=0)
+    idx[...] = both_index.astype(F32).astype(BF16)
 
     def away(facet, col):
         return jnp.logical_or(facet != f, col != c)
@@ -257,13 +258,21 @@
             pltpu.make_async_copy(idx, own_index, own_sem).start()
 
     other = 1 - core
+    def landed(t):
+        for copy in loads[4 * t : 4 * t + 4]:
+            copy.wait()
+
     fill_table(0)
+    fill_second()
+    landed(0)
     fold(0)
-    fill_second()
+    fill_table(1)
     for t in range(chunks):
         if t + 1 < chunks:
+            landed(t + 1)
+            fold(t + 1)
+        if 0 < t < chunks - 1:
             fill_table(t + 1)
-            fold(t + 1)
         here = slice(2 * t * depth, 2 * (t + 1) * depth)
         for index in range(2):
             at = slice(index * cols, (index + 1) * cols)
@@ -272,19 +281,20 @@
                 prod[:, at] = term
             else:
                 prod[:, at] += term
+        if t == chunks // 2 - 1:
+            pl.semaphore_wait(barrier, everyone - 1)
+            each(n_f * n_p, send_index)
 
     finish(bsend, 0)
     swap = pltpu.make_async_remote_copy(
         src_ref=bsend,
-        dst_ref=bands.at[core],
+        dst_ref=bands.at[1],
         send_sem=band_sem.at[0],
         recv_sem=band_sem.at[1],
         device_id={"facet": f, "col": chip * SCOL + other},
     )
 
-    pl.semaphore_wait(barrier, everyone - 1)
     swap.start()
-    each(n_f * n_p, send_index)
 
     def index_from(i, cc):
         pltpu.make_async_copy(idx, idx_all.at[i, cc], irecv_sem.at[i, cc]).wait()
@@ -294,7 +304,7 @@
     sub16 = iota((16, slots), 0)
 
     def prepare(i, cc):
-        block = idx_all[i, cc]
+        block = idx_all[i, cc].astype(F32).astype(jnp.int32)
         cell, frac = block[: 2 * blocks], block[2 * blocks :]
         match = [frac == row for row in range(over)]
         taps = []
@@ -316,20 +326,28 @@
 
         return [window(b, sub16) for b in range(blocks)], [window(blocks + b, sub) for b in range(blocks)]
 
-    finish(bands.at[core], S)
+    finish(bands.at[0], S)
+
+    def shift(h, step=16):
+        for part in range(cols // LANES):
+            near = slice(part * LANES, (part + 1) * LANES)
+            at = slice(h * cols + near.start, h * cols + near.stop)
+            for top in range(0, S, step):
+                re = bands[h, 0, top : top + step, near].astype(F32)
+                im = bands[h, 1, top : top + step, near].astype(F32)
+                for i in range(per):
+                    sc = shift_tab[0, i, 0:1, at]
+                    sd = shift_tab[1, i, 0:1, at]
+                    stacked[i, top : top + step, at] = (re * sc + im * sd).astype(BF16)
+                    stacked[i, S + top : S + top + step, at] = (im * sc - re * sd).astype(BF16)
+
+    shift(0)
     swap.wait_recv()
+    shift(1)
 
     def grid_of(i):
-        for h in range(SCOL):
-            at = slice(h * cols, (h + 1) * cols)
-            sc = shift_tab[0, i, 0:1, at]
-            sd = shift_tab[1, i, 0:1, at]
-            re = bands[h, 0].astype(F32)
-            im = bands[h, 1].astype(F32)
-            stacked[:S, at] = (re * sc + im * sd).astype(BF16)
-            stacked[S:, at] = (im * sc - re * sd).astype(BF16)
         both = lax.dot_general(
-            table2[...], stacked[...], (((1,), (1,)), ((), ())), preferred_element_type=F32
+            table2[...], stacked[i], (((1,), (1,)), ((), ())), preferred_element_type=F32
         )
         re = both[:S, :S] + both[S:, S:]
         im = both[:S, S:] - both[S:, :S]
@@ -475,12 +493,12 @@
             pltpu.VMEM((2, per, 8, SCOL * cols), F32),
             pltpu.VMEM((2, 8, S), F32),
             pltpu.VMEM((2 * S, SCOL * cols), BF16),
-            pltpu.VMEM((2 * S, SCOL * cols), BF16),
+            pltpu.VMEM((per, 2 * S, SCOL * cols), BF16),
             pltpu.VMEM((SCOL, 2, S, cols), BF16),
             pltpu.VMEM((2, S, cols), BF16),
             pltpu.VMEM((per, 2 * S, S), BF16),
-            pltpu.VMEM((4 * blocks, slots), jnp.int32),
-            pltpu.VMEM((per, n_c, 4 * blocks, slots), jnp.int32),
+            pltpu.VMEM((4 * blocks, slots), BF16),
+            pltpu.VMEM((per, n_c, 4 * blocks, slots), BF16),
             pltpu.VMEM((min(n_c, 4), S, blocks * slots), BF16),
             pltpu.VMEM((per, n_c, 2 * blocks, slots), F32),
             pltpu.VMEM((n_f, n_p, 2 * blocks, slots), F32),

time: 28.1 us -> 26.1 us (0.929)
  Pallas kernels: 25.9 us -> 23.9 us
    pallas_call x1, Pallas kernels: 25.9 us -> 23.9 us  [local(): pl.pallas_call(functools.partial(body, dims), out_shape=jax.ShapeDtypeStr...]
where the time goes in v4:
time: 26.1 us; the launch traced here: 25.9 us
  Pallas kernels  23.9 us (92%)
  local copies, waits for them, and re-layouts  1.33 us (5%)
  between operations  0.64 us (2%)
    pallas_call x1, Pallas kernels, local(): pl.pallas_call(functools.partial(body, dims), out_shape=jax.ShapeDtypeStr...  23.9 us
    squeeze x1, local copies, waits for them, and re-layouts, local(): return (vis[0], vis[1])  1.33 us

profile of v4, /device:TPU:0, one launch (start us, length us, event | category | flops | bytes accessed | tf_op | source)
XLA Modules:
  0.0 25.9 jit_solution(4800632535729253521)
XLA Ops:
  0.6 23.9 %shard_map.95 = f32[8,128]{1,0:T(8,128)} custom-call(s32[2]{0:T(128)} %coff_ref.1, s32[4]{0:T(128)} %soff_ref.1, f32[8,16]{1,0:T(8,128)} %bitcast.8, s32[4]{0:T(128)} %bitcast.11, s32[8,128]{1,0:T(8,128)} %bitcast.9, s32[8,128]{1,0:T(8,128)} %bitcast.10, bf16[1,4096,512]{2,1,0:T(8,128)(2,1)} %re_hbm.1, bf16[1,4096,512]{2,1,0:T(8,128)(2,1)} %im_hbm.1), custom_call_target="tpu_custom_call" | custom-call | tf_op jit(solution)/shard_map/pallas_call | solution.py:480
  24.5 1.3 %slice_bitcast_fusion = (f32[1,4,128]{2,1,0:T(4,128)}, f32[1,4,128]{2,1,0:T(4,128)}) fusion(f32[8,128]{1,0:T(8,128)} %shard_map.95), kind=kLoop, calls=%fused_computation | loop fusion | bytes 8192 | tf_op jit(solution)/shard_map/squeeze | solution.py:526

commit v5 on v4

--- a/solution.py
+++ b/solution.py
@@ -90,6 +90,7 @@
     table,
     flip_mat,
     state,
+    jumps,
     prod,
     base,
     shift_tab,
@@ -101,6 +102,11 @@
     cells,
     idx,
     idx_all,
+    kern_vec,
+    tap_buf,
+    cell_buf,
+    row_buf,
+    at_buf,
     weights,
     vsend,
     vrecv,
@@ -157,16 +163,18 @@
         for n, q in enumerate(order):
             for g in range(S // rows):
                 start = coff_ref[q] + g * rows
-                ll = pixels - 1 - 2 * iota((8, LANES), 1)
-                jump = unit((start * (2 * LANES) + 0 * ll) & (wide - 1), wide)
-                jump = times((base[2], base[3]), (jump[0][0:1], jump[1][0:1]))
-                jump = (jump[0], -jump[1])
                 here = slice(n * S + g * rows, n * S + (g + 1) * rows)
                 if t == 0:
+                    ll = pixels - 1 - 2 * iota((8, LANES), 1)
+                    jump = unit((start * (2 * LANES) + 0 * ll) & (wide - 1), wide)
+                    jump = times((base[2], base[3]), (jump[0][0:1], jump[1][0:1]))
+                    jump = (jump[0], -jump[1])
+                    jumps[0, here], jumps[1, here] = jump
                     along = unit((start * ll) & (wide - 1), wide)
                     along = (along[0][0:1] * scale1, along[1][0:1] * scale1)
                     now = times((base[0], base[1]), along)
                 else:
+                    jump = (jumps[0, here], jumps[1, here])
                     now = (state[0, here], state[1, here])
                 for part in range(depth // LANES):
                     lanes = slice(2 * t * depth + part * LANES, 2 * t * depth + (part + 1) * LANES)
@@ -262,6 +270,11 @@
         for copy in loads[4 * t : 4 * t + 4]:
             copy.wait()
 
+    for tap in range(ksize):
+        for step in range(over):
+            kern_vec[tap, step] = jnp.full((2 * blocks, slots), kern_ref[tap, step], F32)
+
+    split = chunks // 2
     fill_table(0)
     fill_second()
     landed(0)
@@ -274,13 +287,14 @@
         if 0 < t < chunks - 1:
             fill_table(t + 1)
         here = slice(2 * t * depth, 2 * (t + 1) * depth)
+        lines = slice(0, S if t >= split else 2 * S)
         for index in range(2):
             at = slice(index * cols, (index + 1) * cols)
-            term = jnp.dot(table[:, here], folded[here, at], preferred_element_type=F32)
+            term = jnp.dot(table[lines, here], folded[here, at], preferred_element_type=F32)
             if t == 0:
-                prod[:, at] = term
+                prod[lines, at] = term
             else:
-                prod[:, at] += term
+                prod[lines, at] += term
         if t == chunks // 2 - 1:
             pl.semaphore_wait(barrier, everyone - 1)
             each(n_f * n_p, send_index)
@@ -303,29 +317,40 @@
 
     sub16 = iota((16, slots), 0)
 
-    def prepare(i, cc):
+    def prepare(i, cc, slot):
         block = idx_all[i, cc].astype(F32).astype(jnp.int32)
-        cell, frac = block[: 2 * blocks], block[2 * blocks :]
-        match = [frac == row for row in range(over)]
-        taps = []
+        frac = block[2 * blocks :]
+        cell_buf[slot] = block[: 2 * blocks]
         for tap in range(ksize):
-            value = jnp.zeros(frac.shape, F32)
-            for row in range(over):
-                value = jnp.where(match[row], kern_ref[tap, row], value)
-            taps.append(value)
+            values = [kern_vec[tap, step] for step in range(over)]
+            bit = 1
+            while len(values) > 1:
+                odd = (frac & bit) != 0
+                values = [jnp.where(odd, high, low) for low, high in zip(values[::2], values[1::2])]
+                bit *= 2
+            tap_buf[slot, tap] = values[0]
 
         def window(b, line):
             size = line.shape[0]
-            lo = cell[b : b + 1] & (size - 1)
+            cell = jnp.broadcast_to(cell_buf[slot, b : b + 1], line.shape)
+            lo = cell & (size - 1)
             turn = (line - lo) & (size - 1)
             value = jnp.zeros(line.shape, F32)
             for tap in range(ksize):
-                value = jnp.where(turn == tap, taps[tap][b : b + 1], value)
-            high = cell[b : b + 1] >> (size.bit_length() - 1)
+                value = jnp.where(turn == tap, tap_buf[slot, tap, b : b + 1], value)
+            high = cell >> (size.bit_length() - 1)
             return value, high + jnp.where(line < lo, 1, 0)
 
-        return [window(b, sub16) for b in range(blocks)], [window(blocks + b, sub) for b in range(blocks)]
-
+        for b in range(blocks):
+            value, at = window(b, sub16)
+            row_buf[slot, b] = value.astype(BF16)
+            at_buf[slot, b] = at.astype(jnp.int16)
+        return [window(blocks + b, sub) for b in range(blocks)]
+
+    here = slice(2 * split * depth, pixels)
+    for index in range(2):
+        at = slice(index * cols, (index + 1) * cols)
+        prod[S:, at] += jnp.dot(table[S:, here], folded[here, at], preferred_element_type=F32)
     finish(bands.at[0], S)
 
     def shift(h, step=16):
@@ -367,10 +392,10 @@
         )
 
     def degrid(i, cc, slot):
-        row, col = prepare(i, cc)
+        col = prepare(i, cc, slot)
         for b in range(blocks):
             lanes = slice(b * slots, (b + 1) * slots)
-            value, at = row[b][0].astype(BF16), row[b][1].astype(jnp.int16)
+            value, at = row_buf[slot, b], at_buf[slot, b]
             for g in range(S // 16):
                 weights[slot, 16 * g : 16 * (g + 1), lanes] = jnp.where(
                     at == jnp.int16(g), value, jnp.zeros_like(value)
@@ -420,6 +445,31 @@
 
         each(n_c // batch, to_owners)
 
+    swap.wait_send()
+
+    def index_sent(step):
+        (rf, target), copy = to_reader(step)
+        if isinstance(step, int) and step > 0:
+            copy.wait_send()
+            return
+
+        @pl.when(away(rf, target))
+        def _():
+            copy.wait_send()
+
+    def vis_sent(step):
+        i, cc = lax.rem(step, per), lax.rem(c + step // per, n_c)
+        if isinstance(step, int) and step >= per:
+            vis_copy(i, cc).wait_send()
+            return
+
+        @pl.when(away(core * per + i, cc))
+        def _():
+            vis_copy(i, cc).wait_send()
+
+    each(n_f * n_p, index_sent)
+    each(per * n_c, vis_sent)
+
     def vis_from(step):
         sf, sp = step // n_p, lax.rem(step, n_p)
         pltpu.make_async_copy(vsend.at[0, 0], vrecv.at[sf, sp], vrecv_sem.at[sf, sp]).wait()
@@ -433,31 +483,6 @@
         live = iota((1, slots), 1) < count_ref[b]
         vis_ref[b : b + 1] = jnp.where(live, acc[b : b + 1], 0.0)
         vis_ref[blocks + b : blocks + b + 1] = jnp.where(live, acc[blocks + b : blocks + b + 1], 0.0)
-
-    swap.wait_send()
-
-    def index_sent(step):
-        (rf, target), copy = to_reader(step)
-        if isinstance(step, int) and step > 0:
-            copy.wait_send()
-            return
-
-        @pl.when(away(rf, target))
-        def _():
-            copy.wait_send()
-
-    def vis_sent(step):
-        i, cc = lax.rem(step, per), lax.rem(c + step // per, n_c)
-        if isinstance(step, int) and step >= per:
-            vis_copy(i, cc).wait_send()
-            return
-
-        @pl.when(away(core * per + i, cc))
-        def _():
-            vis_copy(i, cc).wait_send()
-
-    each(n_f * n_p, index_sent)
-    each(per * n_c, vis_sent)
 
 
 def local(sky_re, sky_im, col_offsets, sub_offsets, kernel, vis_count, cell_index, frac_index):
@@ -472,6 +497,7 @@
     chunks = 4
     per = subs // SCOL
     n_p = n_c // SCOL
+    batch = min(n_c, 4)
     dims = (n_f, n_c, pixels, cols, subs, blocks, slots, chunks, ksize, over)
     smem = pl.BlockSpec(memory_space=pltpu.SMEM)
     vmem = pl.BlockSpec(memory_space=pltpu.VMEM)
@@ -488,6 +514,7 @@
             pltpu.VMEM((2 * S, pixels), BF16),
             pltpu.VMEM((256, 256), BF16),
             pltpu.VMEM((2, 2 * S, LANES), F32),
+            pltpu.VMEM((2, 2 * S, LANES), F32),
             pltpu.VMEM((2 * S, 2 * cols), F32),
             pltpu.VMEM((4, 64, LANES), F32),
             pltpu.VMEM((2, per, 8, SCOL * cols), F32),
@@ -499,7 +526,12 @@
             pltpu.VMEM((per, 2 * S, S), BF16),
             pltpu.VMEM((4 * blocks, slots), BF16),
             pltpu.VMEM((per, n_c, 4 * blocks, slots), BF16),
-            pltpu.VMEM((min(n_c, 4), S, blocks * slots), BF16),
+            pltpu.VMEM((ksize, over, 2 * blocks, slots), F32),
+            pltpu.VMEM((batch, ksize, 2 * blocks, slots), F32),
+            pltpu.VMEM((batch, 2 * blocks, slots), jnp.int32),
+            pltpu.VMEM((batch, blocks, 16, slots), BF16),
+            pltpu.VMEM((batch, blocks, 16, slots), jnp.int16),
+            pltpu.VMEM((batch, S, blocks * slots), BF16),
             pltpu.VMEM((per, n_c, 2 * blocks, slots), F32),
             pltpu.VMEM((n_f, n_p, 2 * blocks, slots), F32),
             dma((chunks, 4)),

time: 26.1 us -> 25 us (0.958)
  Pallas kernels: 23.9 us -> 22.8 us
    pallas_call x1, Pallas kernels: 23.9 us -> 22.8 us  [local(): pl.pallas_call(functools.partial(body, dims), out_shape=jax.ShapeDtypeStr...]
where the time goes in v5:
time: 25 us; the launch traced here: 24.8 us
  Pallas kernels  22.8 us (91%)
  local copies, waits for them, and re-layouts  1.33 us (5%)
  between operations  0.64 us (3%)
    pallas_call x1, Pallas kernels, local(): pl.pallas_call(functools.partial(body, dims), out_shape=jax.ShapeDtypeStr...  22.8 us
    squeeze x1, local copies, waits for them, and re-layouts, local(): return (vis[0], vis[1])  1.33 us

profile of v5, /device:TPU:0, one launch (start us, length us, event | category | flops | bytes accessed | tf_op | source)
XLA Modules:
  0.0 24.8 jit_solution(14207477751161287751)
XLA Ops:
  0.6 22.8 %shard_map.95 = f32[8,128]{1,0:T(8,128)} custom-call(s32[2]{0:T(128)} %coff_ref.1, s32[4]{0:T(128)} %soff_ref.1, f32[8,16]{1,0:T(8,128)} %bitcast.8, s32[4]{0:T(128)} %bitcast.11, s32[8,128]{1,0:T(8,128)} %bitcast.9, s32[8,128]{1,0:T(8,128)} %bitcast.10, bf16[1,4096,512]{2,1,0:T(8,128)(2,1)} %re_hbm.1, bf16[1,4096,512]{2,1,0:T(8,128)(2,1)} %im_hbm.1), custom_call_target="tpu_custom_call" | custom-call | tf_op jit(solution)/shard_map/pallas_call | solution.py:506
  23.5 1.3 %slice_bitcast_fusion = (f32[1,4,128]{2,1,0:T(4,128)}, f32[1,4,128]{2,1,0:T(4,128)}) fusion(f32[8,128]{1,0:T(8,128)} %shard_map.95), kind=kLoop, calls=%fused_computation | loop fusion | bytes 8192 | tf_op jit(solution)/shard_map/squeeze | solution.py:558

commit v6 on v5

--- a/solution.py
+++ b/solution.py
@@ -97,6 +97,7 @@
     turn_tab,
     table2,
     stacked,
+    partial,
     bands,
     bsend,
     cells,
@@ -366,21 +367,28 @@
                     stacked[i, top : top + step, at] = (re * sc + im * sd).astype(BF16)
                     stacked[i, S + top : S + top + step, at] = (im * sc - re * sd).astype(BF16)
 
+    def term_of(i, h):
+        at = slice(h * cols, (h + 1) * cols)
+        return lax.dot_general(
+            table2[:, at], stacked[i, :, at], (((1,), (1,)), ((), ())), preferred_element_type=F32
+        )
+
     shift(0)
+    for i in range(per):
+        partial[i] = term_of(i, 0)
     swap.wait_recv()
     shift(1)
 
     def grid_of(i):
-        both = lax.dot_general(
-            table2[...], stacked[i], (((1,), (1,)), ((), ())), preferred_element_type=F32
-        )
+        both = partial[i] + term_of(i, 1)
         re = both[:S, :S] + both[S:, S:]
         im = both[:S, S:] - both[S:, :S]
         tc, td = turn_tab[0, 0:1], turn_tab[1, 0:1]
         cells[i, :S] = (re * tc + im * td).astype(BF16)
         cells[i, S:] = (im * tc - re * td).astype(BF16)
 
-    each(per, grid_of)
+    for i in range(per):
+        grid_of(i)
 
     def vis_copy(i, cc):
         return pltpu.make_async_remote_copy(
@@ -521,6 +529,7 @@
             pltpu.VMEM((2, 8, S), F32),
             pltpu.VMEM((2 * S, SCOL * cols), BF16),
             pltpu.VMEM((per, 2 * S, SCOL * cols), BF16),
+            pltpu.VMEM((per, 2 * S, 2 * S), F32),
             pltpu.VMEM((SCOL, 2, S, cols), BF16),
             pltpu.VMEM((2, S, cols), BF16),
             pltpu.VMEM((per, 2 * S, S), BF16),

time: 25 us -> 25 us (level)
  no operation moved by 1% of the time
where the time goes in v6:
time: 25 us; the launch traced here: 24.8 us
  Pallas kernels  22.8 us (91%)
  local copies, waits for them, and re-layouts  1.33 us (5%)
  between operations  0.64 us (3%)
    pallas_call x1, Pallas kernels, local(): pl.pallas_call(functools.partial(body, dims), out_shape=jax.ShapeDtypeStr...  22.8 us
    squeeze x1, local copies, waits for them, and re-layouts, local(): return (vis[0], vis[1])  1.33 us

profile of v6, /device:TPU:0, one launch (start us, length us, event | category | flops | bytes accessed | tf_op | source)
XLA Modules:
  0.0 24.8 jit_solution(623896277981564321)
XLA Ops:
  0.6 22.8 %shard_map.95 = f32[8,128]{1,0:T(8,128)} custom-call(s32[2]{0:T(128)} %coff_ref.1, s32[4]{0:T(128)} %soff_ref.1, f32[8,16]{1,0:T(8,128)} %bitcast.8, s32[4]{0:T(128)} %bitcast.11, s32[8,128]{1,0:T(8,128)} %bitcast.9, s32[8,128]{1,0:T(8,128)} %bitcast.10, bf16[1,4096,512]{2,1,0:T(8,128)(2,1)} %re_hbm.1, bf16[1,4096,512]{2,1,0:T(8,128)(2,1)} %im_hbm.1), custom_call_target="tpu_custom_call" | custom-call | tf_op jit(solution)/shard_map/pallas_call | solution.py:514
  23.5 1.3 %slice_bitcast_fusion = (f32[1,4,128]{2,1,0:T(4,128)}, f32[1,4,128]{2,1,0:T(4,128)}) fusion(f32[8,128]{1,0:T(8,128)} %shard_map.95), kind=kLoop, calls=%fused_computation | loop fusion | bytes 8192 | tf_op jit(solution)/shard_map/squeeze | solution.py:567
